TPU v7x, 32 devices: a whole 2x2x4 slice. The times are simulated.
32 devices in a mesh: dp: 8 (over z, y), tensor: 4 (over x, core).
Axes of the slice: x: 2, y: 2, z: 4, core: 2. Of those that a mesh axis runs over, the one named last changes fastest.
Arguments:
- tokens: bfloat16 [2048, 2048], P('dp'), may hold values from -6 to 6
- documents: int32 [8, 256], P('dp'), may hold values from 0 to 7, never falling along the last dimension, each value on 1 to 128 neighbouring positions
- cotangent: bfloat16 [2048, 2048], P('dp'), may hold values from -6 to 6
- qkv_weight: float32 [3, 2048, 2048], P(None, 'dp', 'tensor'), may hold values from -0.1875 to 0.1875
- out_weight: float32 [2048, 2048], P(('tensor', 'dp')), may hold values from -0.25 to 0.25
- lift_weight: float32 [2, 2048, 8192], P(None, 'dp', 'tensor'), may hold values from -0.125 to 0.125
- down_weight: float32 [8192, 2048], P(('tensor', 'dp')), may hold values from -0.0625 to 0.0625
- gains: float32 [2, 2048], P(None, 'dp'), may hold values from 0.5 to 1.5
- qkv_first: float32 [3, 2048, 2048], P(None, 'dp', 'tensor'), may hold values from -3.5 to 3.5
- out_first: float32 [2048, 2048], P(('tensor', 'dp')), may hold values from -3.5 to 3.5
- lift_first: float32 [2, 2048, 8192], P(None, 'dp', 'tensor'), may hold values from -3.5 to 3.5
- down_first: float32 [8192, 2048], P(('tensor', 'dp')), may hold values from -3.5 to 3.5
- gains_first: float32 [2, 2048], P(None, 'dp'), may hold values from -3.5 to 3.5
- qkv_second: float32 [3, 2048, 2048], P(None, 'dp', 'tensor'), may hold values from 0.21038716 to 0.8415486
- out_second: float32 [2048, 2048], P(('tensor', 'dp')), may hold values from 0.21038716 to 0.8415486
- lift_second: float32 [2, 2048, 8192], P(None, 'dp', 'tensor'), may hold values from 0.21038716 to 0.8415486
- down_second: float32 [8192, 2048], P(('tensor', 'dp')), may hold values from 0.21038716 to 0.8415486
- gains_second: float32 [2, 2048], P(None, 'dp'), may hold values from 0.21038716 to 0.8415486
Outputs:
- layer_out: bfloat16 [2048, 2048], P('dp')
- grad_tokens: float32 [2048, 2048], P('dp')
- qkv_new: float32 [3, 2048, 2048], P(None, 'dp', 'tensor')
- out_new: float32 [2048, 2048], P(('tensor', 'dp'))
- lift_new: float32 [2, 2048, 8192], P(None, 'dp', 'tensor')
- down_new: float32 [8192, 2048], P(('tensor', 'dp'))
- gains_new: float32 [2, 2048], P(None, 'dp')
- qkv_moment: float32 [3, 2048, 2048], P(None, 'dp', 'tensor')
- out_moment: float32 [2048, 2048], P(('tensor', 'dp'))
- lift_moment: float32 [2, 2048, 8192], P(None, 'dp', 'tensor')
- down_moment: float32 [8192, 2048], P(('tensor', 'dp'))
- gains_moment: float32 [2, 2048], P(None, 'dp')
- qkv_variance: float32 [3, 2048, 2048], P(None, 'dp', 'tensor')
- out_variance: float32 [2048, 2048], P(('tensor', 'dp'))
- lift_variance: float32 [2, 2048, 8192], P(None, 'dp', 'tensor')
- down_variance: float32 [8192, 2048], P(('tensor', 'dp'))
- gains_variance: float32 [2, 2048], P(None, 'dp')
- grad_norm: float32 [], replicated
Inputs may be any that keep to these rules, and one draw needn't show every extreme that they name: Each row of documents is one sequence: ids never fall along the row, and each id is one document of 1 to 128 tokens.
All inputs are finite; a program needn't handle non-finite values.
Results may differ from a plain program's by a relative error of at most 0.015.
The roundings to bfloat16 on the way count: a program that leaves them out, or rounds other values in their place, can miss the bound.
Values may be sent and summed in bfloat16 or wider, within the bound.
No kernel may reach another device: no remote copies, remote signals or barrier semaphores. Data moves between devices by JAX's collectives and lax.ppermute only.
A program may use at most 256 MiB of HBM per device.

v0:
```python
import math
import jax
import jax.numpy as jnp
from jax import lax
from jax.sharding import PartitionSpec as P

HD = 128
STEP = 10
CLIP_NORM = 16384
norm_eps = 1e-05
beta_one = 0.9
beta_two = 0.95
adam_eps = 1e-08
rate_matrix = 0.02
rate_gain = 0.5
decay_matrix = 0.1


def norm_forward(rows, gain):
    inverse = lax.rsqrt(jnp.mean(rows * rows, axis=-1, keepdims=True) + norm_eps)
    scaled = rows * inverse
    return (scaled, inverse, (scaled * gain).astype(jnp.bfloat16))


def norm_backward(incoming, scaled, inverse, gain):
    grad_gain = jnp.sum(incoming * scaled, axis=0)
    weighted = incoming * gain
    grad_rows = inverse * (weighted - scaled * jnp.mean(weighted * scaled, axis=-1, keepdims=True))
    return (grad_gain, grad_rows)


def block_probs(queries, keys, doc_row, start, block, scale, offset):
    length = keys.shape[0]
    query_pos = start + jnp.arange(block, dtype=jnp.int32)
    key_pos = jnp.arange(length, dtype=jnp.int32)
    allowed = (query_pos[:, None] >= key_pos[None, :]) & (doc_row[:, None] == doc_row[None, :])
    scores = (
        jnp.einsum("qhd,khd->hqk", queries, keys, preferred_element_type=jnp.float32) * scale
        + offset
    )
    probs = jnp.where(allowed[None], jax.nn.sigmoid(scores), 0.0)
    return (queries, probs)


def adam_step(weight, first, second, grad, factor, rate, decay):
    clipped = grad * factor
    moment = beta_one * first + (1.0 - beta_one) * clipped
    variance = beta_two * second + (1.0 - beta_two) * clipped * clipped
    corr_one = 1.0 - beta_one**STEP
    corr_two = 1.0 - beta_two**STEP
    update = moment / corr_one / (jnp.sqrt(variance / corr_two) + adam_eps)
    return (weight - rate * (update + decay * weight), moment, variance)


def on_device(
    tokens,
    documents,
    cotangent,
    qkv_weight,
    out_weight,
    lift_weight,
    down_weight,
    gains,
    qkv_first,
    out_first,
    lift_first,
    down_first,
    gains_first,
    qkv_second,
    out_second,
    lift_second,
    down_second,
    gains_second,
):
    bf16 = jnp.bfloat16
    f32 = jnp.float32
    w_qkv, w_out, w_lift, w_down, w_gains = (
        lax.all_gather(qkv_weight.astype(bf16), "dp", axis=1, tiled=True),
        lax.all_gather(out_weight.astype(bf16), "dp", axis=0, tiled=True),
        lax.all_gather(lift_weight.astype(bf16), "dp", axis=1, tiled=True),
        lax.all_gather(down_weight.astype(bf16), "dp", axis=0, tiled=True),
        lax.all_gather(gains.astype(bf16), "dp", axis=1, tiled=True),
    )
    length = tokens.shape[0]
    local_width = w_qkv.shape[2]
    heads = local_width // HD
    block = min(512, length)
    blocks = length // block
    scale = 1.0 / math.sqrt(HD)
    offset = -math.log(length)
    doc_row = documents[0]
    gain_one = w_gains[0].astype(f32)
    gain_two = w_gains[1].astype(f32)
    x_rows = tokens.astype(f32)
    scaled_one, inverse_one, normed_one = norm_forward(x_rows, gain_one)
    project = jnp.einsum("td,cde->cte", normed_one, w_qkv, preferred_element_type=f32).astype(bf16)
    queries = project[0].reshape(length, heads, HD)
    keys = project[1].reshape(length, heads, HD)
    values = project[2].reshape(length, heads, HD)

    def attend(index):
        start = index * block
        query_block, probs = block_probs(queries, keys, doc_row, start, block, scale, offset)
        return jnp.einsum(
            "hqk,khd->qhd", probs.astype(bf16), values, preferred_element_type=f32
        ).astype(bf16)

    attended = lax.map(attend, jnp.arange(blocks, dtype=jnp.int32)).reshape(length, local_width)
    branch = lax.psum(jnp.dot(attended, w_out, preferred_element_type=f32), "tensor")
    middle = x_rows + branch
    scaled_two, inverse_two, normed_two = norm_forward(middle, gain_two)
    gate_up = jnp.einsum("td,cde->cte", normed_two, w_lift, preferred_element_type=f32)
    gate = gate_up[0]
    upward = gate_up[1]
    sigma = jax.nn.sigmoid(gate)
    hidden = (gate * sigma * upward).astype(bf16)
    feed = lax.psum(
        jnp.dot(hidden, w_down, preferred_element_type=f32).astype(jnp.bfloat16), "tensor"
    ).astype(jnp.float32)
    layer_out = (middle + feed).astype(bf16)
    grad_incoming = cotangent.astype(f32)
    grad_down = jnp.einsum("tf,td->fd", hidden, cotangent, preferred_element_type=f32)
    grad_hidden = jnp.einsum("td,fd->tf", cotangent, w_down, preferred_element_type=f32)
    grad_gate = (grad_hidden * upward * sigma * (1.0 + gate * (1.0 - sigma))).astype(bf16)
    grad_up = (grad_hidden * gate * sigma).astype(bf16)
    grad_pair = jnp.stack([grad_gate, grad_up])
    grad_lift = jnp.einsum("td,ctf->cdf", normed_two, grad_pair, preferred_element_type=f32)
    back_two = lax.psum(
        jnp.einsum("ctf,cdf->td", grad_pair, w_lift, preferred_element_type=f32), "tensor"
    )
    grad_gain_two, grad_mid_norm = norm_backward(back_two, scaled_two, inverse_two, gain_two)
    grad_mid = grad_incoming + grad_mid_norm
    grad_branch = grad_mid.astype(bf16)
    grad_out = jnp.einsum("te,td->ed", attended, grad_branch, preferred_element_type=f32)
    grad_attended = jnp.einsum("td,ed->te", grad_branch, w_out, preferred_element_type=f32).astype(
        bf16
    )
    grad_heads = grad_attended.reshape(length, heads, HD)

    def attend_back(carry, index):
        grad_keys, grad_values = carry
        start = index * block
        query_block, probs = block_probs(queries, keys, doc_row, start, block, scale, offset)
        grad_probs = jnp.einsum("qhd,khd->hqk", grad_heads, values, preferred_element_type=f32)
        grad_scores = (grad_probs * probs * (1.0 - probs)).astype(bf16)
        grad_query = (
            jnp.einsum("hqk,khd->qhd", grad_scores, keys, preferred_element_type=f32) * scale
        )
        grad_keys = (
            grad_keys
            + jnp.einsum("hqk,qhd->khd", grad_scores, query_block, preferred_element_type=f32)
            * scale
        )
        grad_values = grad_values + jnp.einsum(
            "hqk,qhd->khd", probs.astype(bf16), grad_heads, preferred_element_type=f32
        )
        return ((grad_keys, grad_values), grad_query)

    zeros_kv = jnp.zeros((length, heads, HD), f32)
    (grad_keys, grad_values), grad_queries = lax.scan(
        attend_back, (zeros_kv, zeros_kv), jnp.arange(blocks, dtype=jnp.int32)
    )
    grad_project = jnp.stack(
        [
            grad_queries.reshape(length, local_width),
            grad_keys.reshape(length, local_width),
            grad_values.reshape(length, local_width),
        ]
    ).astype(bf16)
    grad_qkv = jnp.einsum("td,cte->cde", normed_one, grad_project, preferred_element_type=f32)
    back_one = lax.psum(
        jnp.einsum("cte,cde->td", grad_project, w_qkv, preferred_element_type=f32), "tensor"
    )
    grad_gain_one, grad_x_norm = norm_backward(back_one, scaled_one, inverse_one, gain_one)
    grad_tokens = grad_mid + grad_x_norm
    grad_gains = jnp.stack([grad_gain_one, grad_gain_two])
    red_qkv, red_out, red_lift, red_down, red_gains = (
        lax.psum_scatter(grad_qkv, "dp", scatter_dimension=1, tiled=True),
        lax.psum_scatter(grad_out, "dp", scatter_dimension=0, tiled=True),
        lax.psum_scatter(grad_lift, "dp", scatter_dimension=1, tiled=True),
        lax.psum_scatter(grad_down, "dp", scatter_dimension=0, tiled=True),
        lax.psum_scatter(grad_gains, "dp", scatter_dimension=1, tiled=True),
    )
    local_total = (
        jnp.sum(red_qkv * red_qkv)
        + jnp.sum(red_out * red_out)
        + jnp.sum(red_lift * red_lift)
        + jnp.sum(red_down * red_down)
        + jnp.sum(red_gains * red_gains) / lax.axis_size("tensor")
    )
    total = lax.psum(local_total, ("dp", "tensor"))
    grad_norm = jnp.sqrt(total)
    factor = CLIP_NORM / jnp.maximum(grad_norm, CLIP_NORM)
    qkv_new, qkv_moment, qkv_variance = adam_step(
        qkv_weight, qkv_first, qkv_second, red_qkv, factor, rate_matrix, decay_matrix
    )
    out_new, out_moment, out_variance = adam_step(
        out_weight, out_first, out_second, red_out, factor, rate_matrix, decay_matrix
    )
    lift_new, lift_moment, lift_variance = adam_step(
        lift_weight, lift_first, lift_second, red_lift, factor, rate_matrix, decay_matrix
    )
    down_new, down_moment, down_variance = adam_step(
        down_weight, down_first, down_second, red_down, factor, rate_matrix, decay_matrix
    )
    gains_new, gains_moment, gains_variance = adam_step(
        gains, gains_first, gains_second, red_gains, factor, rate_gain, 0.0
    )
    return (
        layer_out,
        grad_tokens,
        qkv_new,
        out_new,
        lift_new,
        down_new,
        gains_new,
        qkv_moment,
        out_moment,
        lift_moment,
        down_moment,
        gains_moment,
        qkv_variance,
        out_variance,
        lift_variance,
        down_variance,
        gains_variance,
        grad_norm,
    )


def solution(mesh):
    placed = (
        P("dp", None),
        P("dp", None),
        P("dp", None),
        P(None, "dp", "tensor"),
        P(("tensor", "dp"), None),
        P(None, "dp", "tensor"),
        P(("tensor", "dp"), None),
        P(None, "dp"),
        P(None, "dp", "tensor"),
        P(("tensor", "dp"), None),
        P(None, "dp", "tensor"),
        P(("tensor", "dp"), None),
        P(None, "dp"),
        P(None, "dp", "tensor"),
        P(("tensor", "dp"), None),
        P(None, "dp", "tensor"),
        P(("tensor", "dp"), None),
        P(None, "dp"),
    )
    return jax.shard_map(
        on_device,
        mesh=mesh,
        in_specs=placed,
        out_specs=(
            P("dp", None),
            P("dp", None),
            P(None, "dp", "tensor"),
            P(("tensor", "dp"), None),
            P(None, "dp", "tensor"),
            P(("tensor", "dp"), None),
            P(None, "dp"),
            P(None, "dp", "tensor"),
            P(("tensor", "dp"), None),
            P(None, "dp", "tensor"),
            P(("tensor", "dp"), None),
            P(None, "dp"),
            P(None, "dp", "tensor"),
            P(("tensor", "dp"), None),
            P(None, "dp", "tensor"),
            P(("tensor", "dp"), None),
            P(None, "dp"),
            P(),
        ),
        check_vma=False,
    )
```

profile of v0, /device:TPU:0, one launch (start us, length us, event | category | flops | bytes accessed | tf_op | source)
XLA Modules:
  0.0 2062.5 jit_solution(4781406800349877402)
XLA Ops:
  7.3 2.5 convert_element_type.82
  10.7 22.7 %all_gather.15 = bf16[2,2048]{1,0:T(2,128)(2,1)S(1)} all-gather(bf16[2,256]{1,0:T(2,128)(2,1)S(1)} %convert_element_type.80), channel_id=1, replica_groups=mesh['dp'=8,'tensor'=4] {'dp'}, dimensions={1}, use_global_device_ids=true | all-gather | bytes 9216 | tf_op jit(solution)/shard_map/all_gather | solution.py:82
  33.8 78.4 %all-gather.5.cloned.1.call-done = bf16[3,2048,512]{2,1,0:T(8,128)(2,1)} async-done(((bf16[3,256,512]{2,1,0:T(8,128)(2,1)}), bf16[3,2048,512]{2,1,0:T(8,128)(2,1)}) %all-gather.5.cloned.1.call-update) | async-done | bytes 6291472 | tf_op jit(solution)/shard_map/all_gather | solution.py:78
  112.3 4.6 fusion.22
  119.3 43.0 %all-gather.7.cloned.1.call-done = bf16[512,2048]{1,0:T(8,128)(2,1)} async-done(((bf16[64,2048]{1,0:T(8,128)(2,1)}), bf16[512,2048]{1,0:T(8,128)(2,1)}) %all-gather.7.cloned.1.call-update) | async-done | bytes 2097168 | tf_op jit(solution)/shard_map/all_gather | solution.py:79
  162.3 3.6 fusion.53
  166.0 3.8 convert_element_type.90
  169.9 1.6 copy-done.6
  173.0 43.1 %all-reduce.5.cloned.1.call-done = f32[256,2048]{1,0:T(8,128)} async-done(((f32[256,2048]{1,0:T(8,128)}), f32[256,2048]{1,0:T(8,128)}) %all-reduce.5.cloned.1.call-update) | async-done | bytes 2097168 | tf_op jit(solution)/shard_map/psum | solution.py:109
  216.1 1.9 multiply_reduce_fusion.4
  218.0 228.0 %all-gather.9.cloned.1.call-done = bf16[2,2048,2048]{2,1,0:T(8,128)(2,1)} async-done(((bf16[2,256,2048]{2,1,0:T(8,128)(2,1)}), bf16[2,2048,2048]{2,1,0:T(8,128)(2,1)}) %all-gather.9.cloned.1.call-update) | async-done | bytes 16777232 | tf_op jit(solution)/shard_map/all_gather | solution.py:80
  446.0 10.2 convolution_bitcast_fusion.2
  456.3 115.0 %all-gather.11.cloned.1.call-done = bf16[2048,2048]{1,0:T(8,128)(2,1)} async-done(((bf16[256,2048]{1,0:T(8,128)(2,1)}), bf16[2048,2048]{1,0:T(8,128)(2,1)}) %all-gather.11.cloned.1.call-update) | async-done | bytes 8388624 | tf_op jit(solution)/shard_map/all_gather | solution.py:81
  571.3 9.7 fusion.28
  580.9 12.3 convolution_bitcast_fusion.4
  593.3 7.1 convolution_convert_fusion
  600.9 42.0 %all-reduce.9.cloned.1.call-done = f32[256,2048]{1,0:T(8,128)} async-done(((f32[256,2048]{1,0:T(8,128)}), f32[256,2048]{1,0:T(8,128)}) %all-reduce.9.cloned.1.call-update) | async-done | bytes 2097168 | tf_op jit(solution)/shard_map/psum | solution.py:128
  643.0 2.2 multiply_reduce_fusion.1
  645.1 37.2 %all-reduce.7.cloned.1.call-done = bf16[256,2048]{1,0:T(8,128)(2,1)} async-done(((bf16[256,2048]{1,0:T(8,128)(2,1)}), bf16[256,2048]{1,0:T(8,128)(2,1)}) %all-reduce.7.cloned.1.call-update) | async-done | bytes 1048592 | tf_op jit(solution)/shard_map/psum | solution.py:117
  682.3 4.0 multiply_add_fusion.2
  686.3 1.3 copy-done
  687.6 1.5 convolution_convert_fusion.3
  689.1 1.8 copy.96
  690.8 2.4 convolution_convert_fusion.2
  693.2 1.4 fusion.21
  696.6 1.8 copy.73
  698.4 1.8 copy.72
  700.2 1.8 copy.71
  701.9 6.2 convolution_bitcast_fusion.3
  708.2 52.0 %all-reduce.11.cloned.1.call-done = f32[256,2048]{1,0:T(8,128)} async-done(((f32[256,2048]{1,0:T(8,128)}), f32[256,2048]{1,0:T(8,128)}) %all-reduce.11.cloned.1.call-update) | async-done | bytes 2097168 | tf_op jit(solution)/shard_map/psum | solution.py:171
  760.2 2.3 fusion.10
  762.4 1.3 copy.92
  763.9 4.3 fusion.32
  769.1 7.5 convolution_bitcast_fusion.1
  776.7 9.7 fusion.54
  786.6 15.0 convolution_bitcast_fusion
  801.6 1.4 copy-done.9
  803.0 1.6 copy.79
  804.6 5.5 copy.83
  810.1 1.6 copy.74
  811.7 3.0 copy.77
  814.7 5.4 copy.80
  820.1 5.4 copy.81
  825.5 3.0 reduce-scatter.16.cloned.1.call-done
  830.7 89.1 %reduce-scatter.10.cloned.1.call-done = f32[64,2048]{1,0:T(8,128)} async-done(((f32[512,2048]{1,0:T(8,128)}), f32[64,2048]{1,0:T(8,128)}) %reduce-scatter.10.cloned.1.call-update) | async-done | bytes 524304 | tf_op jit(solution)/shard_map/reduce_scatter | solution.py:179
  919.8 1.8 multiply_reduce_fusion.6
  921.6 209.4 %reduce-scatter.8.cloned.1.call-done = f32[3,256,512]{1,2,0:T(8,128)} async-done(((f32[3,2048,512]{1,2,0:T(8,128)}), f32[3,256,512]{1,2,0:T(8,128)}) %reduce-scatter.8.cloned.1.call-update) | async-done | bytes 1572880 | tf_op jit(solution)/shard_map/reduce_scatter | solution.py:178
  1131.0 2.4 multiply_reduce_fusion.5
  1134.7 279.3 %reduce-scatter.14.cloned.1.call-done = f32[256,2048]{1,0:T(8,128)} async-done(((f32[2048,2048]{1,0:T(8,128)}), f32[256,2048]{1,0:T(8,128)}) %reduce-scatter.14.cloned.1.call-update) | async-done | bytes 2097168 | tf_op jit(solution)/shard_map/reduce_scatter | solution.py:181
  1413.9 2.7 multiply_reduce_fusion.2
  1416.7 538.9 %reduce-scatter.12.cloned.1.call-done = f32[2,256,2048]{1,2,0:T(8,128)} async-done(((f32[2,2048,2048]{1,2,0:T(8,128)}), f32[2,256,2048]{1,2,0:T(8,128)}) %reduce-scatter.12.cloned.1.call-update) | async-done | bytes 4194320 | tf_op jit(solution)/shard_map/reduce_scatter | solution.py:180
  1955.5 3.9 multiply_reduce_fusion
  1960.7 3.5 fusion.9
  1964.2 39.5 %psum.39 = f32[]{:T(128)} all-reduce(f32[]{:T(128)S(6)} %add.183), channel_id=1, replica_groups=mesh['dp'=8,'tensor'=4] {'dp','tensor'}, use_global_device_ids=true, to_apply=%region_20.21 | all-reduce | flops 1 | bytes 8 | tf_op jit(solution)/shard_map/psum | solution.py:191
  2004.4 5.7 multiply_subtract_fusion.2
  2010.1 3.0 copy.84
  2013.1 11.3 multiply_subtract_fusion
  2024.5 5.3 copy.85
  2029.8 3.0 copy.86
  2032.8 5.3 copy.87
  2038.2 1.6 copy.88
  2039.8 5.5 copy.89
  2046.0 2.6 multiply_subtract_fusion.3
  2048.6 6.1 multiply_subtract_fusion.1
  (93 shorter events, 11.5 us)
Async XLA Ops:
  7.2 2.7 copy-start.11
  7.2 3.5 copy-start.20
  7.2 26.2 %copy-start.2 = (bf16[256,2048]{1,0:T(8,128)(2,1)S(1)}, bf16[256,2048]{1,0:T(8,128)(2,1)}, u32[]{:S(2)}) copy-start(bf16[256,2048]{1,0:T(8,128)(2,1)} %param.18) | copy-start | bytes 3145732
  7.2 26.5 %copy-start.21 = (s32[1,256]{1,0:T(1,128)S(1)}, s32[1,256]{1,0:T(1,128)}, u32[]{:S(2)}) copy-start(s32[1,256]{1,0:T(1,128)} %param.19) | copy-start | bytes 3076
  7.2 105.0 %all-gather.5.cloned.1.call-start = ((), (), s32[]{:S(2)}) async-start(), calls=%async_computation.5 | async-start | bytes 7077888 | tf_op jit(solution)/shard_map/all_gather | solution.py:78
  9.8 152.5 %all-gather.7.cloned.1.call-start = ((), (), s32[]{:S(2)}) async-start(), calls=%async_computation.6 | async-start | bytes 2359296 | tf_op jit(solution)/shard_map/all_gather | solution.py:79
  10.6 205.5 %all-reduce.5.cloned.1.call-start = ((), (), s32[]{:S(2)}) async-start(), calls=%async_computation.7 | async-start | bytes 4194304 | tf_op jit(solution)/shard_map/psum | solution.py:109
  117.1 0.8 copy-start.16
  117.2 0.7 copy-start.18
  117.3 0.7 copy-start.10
  118.0 1.0 copy-start.3
  166.0 280.1 %all-gather.9.cloned.1.call-start = ((), (), s32[]{:S(2)}) async-start(), calls=%async_computation.8 | async-start | bytes 18874368 | tf_op jit(solution)/shard_map/all_gather | solution.py:80
  169.9 1.7 copy-start.6
  169.9 401.4 %all-gather.11.cloned.1.call-start = ((), (), s32[]{:S(2)}) async-start(), calls=%async_computation.9 | async-start | bytes 9437184 | tf_op jit(solution)/shard_map/all_gather | solution.py:81
  172.7 470.3 %all-reduce.9.cloned.1.call-start = ((), (), s32[]{:S(2)}) async-start(), calls=%async_computation.11 | async-start | bytes 4194304 | tf_op jit(solution)/shard_map/psum | solution.py:128
  593.2 89.0 %all-reduce.7.cloned.1.call-start = ((), (), s32[]{:S(2)}) async-start(), calls=%async_computation.10 | async-start | bytes 2097152 | tf_op jit(solution)/shard_map/psum | solution.py:117
  600.4 159.8 %all-reduce.11.cloned.1.call-start = ((), (), s32[]{:S(2)}) async-start(), calls=%async_computation.12 | async-start | bytes 4194304 | tf_op jit(solution)/shard_map/psum | solution.py:171
  682.3 5.3 copy-start.5
  686.3 1.3 copy-start
  690.8 2.4 copy-start.4
  690.8 3.8 copy-start.17
  690.8 4.7 copy-start.19
  708.2 120.3 %reduce-scatter.16.cloned.1.call-start = ((), (), s32[]{:S(2)}) async-start(), calls=%async_computation.17 | async-start | bytes 1179648
  763.8 156.0 %reduce-scatter.10.cloned.1.call-start = ((), (), s32[]{:S(2)}) async-start(), calls=%async_computation.14 | async-start | bytes 4718592 | tf_op jit(solution)/shard_map/reduce_scatter | solution.py:179
  768.2 0.9 copy-start.15
  768.2 362.7 %reduce-scatter.8.cloned.1.call-start = ((), (), s32[]{:S(2)}) async-start(), calls=%async_computation.13 | async-start | bytes 14155776 | tf_op jit(solution)/shard_map/reduce_scatter | solution.py:178
  776.6 637.3 %reduce-scatter.14.cloned.1.call-start = ((), (), s32[]{:S(2)}) async-start(), calls=%async_computation.16 | async-start | bytes 18874368 | tf_op jit(solution)/shard_map/reduce_scatter | solution.py:181
  786.4 1169.2 %reduce-scatter.12.cloned.1.call-start = ((), (), s32[]{:S(2)}) async-start(), calls=%async_computation.15 | async-start | bytes 37748736 | tf_op jit(solution)/shard_map/reduce_scatter | solution.py:180
  801.6 1.4 copy-start.9
  804.6 5.5 copy-start.14
  1416.7 544.0 %copy-start.1 = (f32[256,2048]{1,0:T(8,128)S(1)}, f32[256,2048]{1,0:T(8,128)}, u32[]{:S(2)}) copy-start(f32[256,2048]{1,0:T(8,128)} %copy-done) | copy-start | bytes 6291460
  2039.8 5.5 copy-start.22
  2039.8 5.5 copy-start.23
  2039.8 6.1 copy-start.12
  2039.8 6.1 copy-start.13
  2039.8 8.8 copy-start.8
  2045.3 3.3 copy-start.7
Sparse Core Ops, SparseCore 0:
  10.8 101.4 all-gather.4
  115.0 47.3 all-gather.6
  166.1 49.9 all-reduce.4
  218.7 227.3 all-gather.8
  448.6 122.6 all-gather.10
  593.4 49.5 all-reduce.8
  645.9 36.3 all-reduce.6
  708.3 51.8 all-reduce.10
  764.2 64.2 reduce-scatter.15
  832.5 87.2 reduce-scatter.9
  923.4 207.4 reduce-scatter.7
  1134.6 279.2 reduce-scatter.13
  1417.7 537.7 reduce-scatter.11
where the time goes:
time: 2070 us; the launch traced here: 2060 us
  waiting for transfers between devices  1760 us (85%)
  matrix products  98 us (5%)
  local copies, waits for them, and re-layouts  62.6 us (3%)
  blocking collectives  62.2 us (3%)
  other arithmetic  60.2 us (3%)
    reduce_scatter x1, waiting for transfers between devices, on_device(): lax.psum_scatter(grad_lift, 'dp', scatter_dimension=1, tiled=True)  539 us
    reduce_scatter x1, waiting for transfers between devices, on_device(): lax.psum_scatter(grad_down, 'dp', scatter_dimension=0, tiled=True)  279 us
    all_gather x1, waiting for transfers between devices, on_device(): lax.all_gather(lift_weight.astype(bf16), 'dp', axis=1, tiled=True)  228 us
    reduce_scatter x1, waiting for transfers between devices, on_device(): lax.psum_scatter(grad_qkv, 'dp', scatter_dimension=1, tiled=True)  209 us
    all_gather x1, waiting for transfers between devices, on_device(): lax.all_gather(down_weight.astype(bf16), 'dp', axis=0, tiled=True)  115 us
    reduce_scatter x1, waiting for transfers between devices, on_device(): lax.psum_scatter(grad_out, 'dp', scatter_dimension=0, tiled=True)  89.1 us
    all_gather x1, waiting for transfers between devices, on_device(): lax.all_gather(qkv_weight.astype(bf16), 'dp', axis=1, tiled=True)  78.4 us
    unnamed x62, local copies, waits for them, and re-layouts  55.1 us
  transfers between devices with their start and end apart: 13, of which 13 were waited for; matrix products, arithmetic and copies ran while one was open for 5% of the time, Pallas kernels for 0%

commit v1 on v0

--- a/solution.py
+++ b/solution.py
@@ -125,8 +125,11 @@
     grad_up = (grad_hidden * gate * sigma).astype(bf16)
     grad_pair = jnp.stack([grad_gate, grad_up])
     grad_lift = jnp.einsum("td,ctf->cdf", normed_two, grad_pair, preferred_element_type=f32)
-    back_two = lax.psum(
-        jnp.einsum("ctf,cdf->td", grad_pair, w_lift, preferred_element_type=f32), "tensor"
+    back_two = jnp.sum(
+        lax.all_gather(
+            jnp.einsum("ctf,cdf->td", grad_pair, w_lift, preferred_element_type=f32), "tensor"
+        ),
+        axis=0,
     )
     grad_gain_two, grad_mid_norm = norm_backward(back_two, scaled_two, inverse_two, gain_two)
     grad_mid = grad_incoming + grad_mid_norm

time: 2070 us -> 2070 us (level)
    all_gather x0 -> x1, waiting for transfers between devices: none -> 48.9 us  [on_device(): lax.all_gather(jnp.einsum('ctf,cdf->td', grad_pair, w_lift, preferred_ele...]
    psum x1 -> x0, waiting for transfers between devices: 42 us -> none  [on_device(): lax.psum(jnp.einsum('ctf,cdf->td', grad_pair, w_lift, preferred_element_t...]
where the time goes in v1:
time: 2070 us
  waiting for transfers between devices  1760 us (85%)
  matrix products  98 us (5%)
  other arithmetic  65.9 us (3%)
  local copies, waits for them, and re-layouts  62.6 us (3%)
  blocking collectives  62.2 us (3%)
    reduce_scatter x1, waiting for transfers between devices, on_device(): lax.psum_scatter(grad_lift, 'dp', scatter_dimension=1, tiled=True)  538 us
    reduce_scatter x1, waiting for transfers between devices, on_device(): lax.psum_scatter(grad_down, 'dp', scatter_dimension=0, tiled=True)  282 us
    all_gather x1, waiting for transfers between devices, on_device(): lax.all_gather(lift_weight.astype(bf16), 'dp', axis=1, tiled=True)  228 us
    reduce_scatter x1, waiting for transfers between devices, on_device(): lax.psum_scatter(grad_qkv, 'dp', scatter_dimension=1, tiled=True)  208 us
    all_gather x1, waiting for transfers between devices, on_device(): lax.all_gather(down_weight.astype(bf16), 'dp', axis=0, tiled=True)  115 us
    reduce_scatter x1, waiting for transfers between devices, on_device(): lax.psum_scatter(grad_out, 'dp', scatter_dimension=0, tiled=True)  89.2 us
    all_gather x1, waiting for transfers between devices, on_device(): lax.all_gather(qkv_weight.astype(bf16), 'dp', axis=1, tiled=True)  78.4 us
    unnamed x62, local copies, waits for them, and re-layouts  55.1 us
  transfers between devices with their start and end apart: 13, of which 13 were waited for; matrix products, arithmetic and copies ran while one was open for 5% of the time, Pallas kernels for 0%

profile of v1, /device:TPU:0, one launch (start us, length us, event | category | flops | bytes accessed | tf_op | source)
XLA Modules:
  0.0 2069.6 jit_solution(2029839334260526096)
XLA Ops:
  7.3 2.5 convert_element_type.82
  10.7 22.7 %all_gather.21 = bf16[2,2048]{1,0:T(2,128)(2,1)S(1)} all-gather(bf16[2,256]{1,0:T(2,128)(2,1)S(1)} %convert_element_type.80), channel_id=1, replica_groups=mesh['dp'=8,'tensor'=4] {'dp'}, dimensions={1}, use_global_device_ids=true | all-gather | bytes 9216 | tf_op jit(solution)/shard_map/all_gather | solution.py:82
  33.8 78.4 %all-gather.7.cloned.1.call-done = bf16[3,2048,512]{2,1,0:T(8,128)(2,1)} async-done(((bf16[3,256,512]{2,1,0:T(8,128)(2,1)}), bf16[3,2048,512]{2,1,0:T(8,128)(2,1)}) %all-gather.7.cloned.1.call-update) | async-done | bytes 6291472 | tf_op jit(solution)/shard_map/all_gather | solution.py:78
  112.3 4.6 fusion.22
  119.3 43.0 %all-gather.9.cloned.1.call-done = bf16[512,2048]{1,0:T(8,128)(2,1)} async-done(((bf16[64,2048]{1,0:T(8,128)(2,1)}), bf16[512,2048]{1,0:T(8,128)(2,1)}) %all-gather.9.cloned.1.call-update) | async-done | bytes 2097168 | tf_op jit(solution)/shard_map/all_gather | solution.py:79
  162.3 3.6 fusion.53
  166.0 3.8 convert_element_type.90
  169.9 1.6 copy-done.6
  173.0 43.1 %all-reduce.4.cloned.1.call-done = f32[256,2048]{1,0:T(8,128)} async-done(((f32[256,2048]{1,0:T(8,128)}), f32[256,2048]{1,0:T(8,128)}) %all-reduce.4.cloned.1.call-update) | async-done | bytes 2097168 | tf_op jit(solution)/shard_map/psum | solution.py:109
  216.1 1.9 multiply_reduce_fusion.4
  218.0 228.0 %all-gather.11.cloned.1.call-done = bf16[2,2048,2048]{2,1,0:T(8,128)(2,1)} async-done(((bf16[2,256,2048]{2,1,0:T(8,128)(2,1)}), bf16[2,2048,2048]{2,1,0:T(8,128)(2,1)}) %all-gather.11.cloned.1.call-update) | async-done | bytes 16777232 | tf_op jit(solution)/shard_map/all_gather | solution.py:80
  446.0 10.2 convolution_bitcast_fusion.2
  456.3 115.0 %all-gather.13.cloned.1.call-done = bf16[2048,2048]{1,0:T(8,128)(2,1)} async-done(((bf16[256,2048]{1,0:T(8,128)(2,1)}), bf16[2048,2048]{1,0:T(8,128)(2,1)}) %all-gather.13.cloned.1.call-update) | async-done | bytes 8388624 | tf_op jit(solution)/shard_map/all_gather | solution.py:81
  571.3 9.7 fusion.28
  580.9 12.3 convolution_bitcast_fusion.4
  593.3 7.0 convolution_convert_fusion
  600.9 48.9 %all-gather.15.cloned.1.call-done = f32[1024,2048]{1,0:T(8,128)} async-done(((f32[256,2048]{1,0:T(8,128)}), f32[1024,2048]{1,0:T(8,128)}) %all-gather.15.cloned.1.call-update) | async-done | bytes 8388624 | tf_op jit(solution)/shard_map/all_gather | solution.py:129
  649.8 5.7 reduce_sum.110
  655.5 2.2 multiply_reduce_fusion.1
  657.7 31.4 %all-reduce.6.cloned.1.call-done = bf16[256,2048]{1,0:T(8,128)(2,1)} async-done(((bf16[256,2048]{1,0:T(8,128)(2,1)}), bf16[256,2048]{1,0:T(8,128)(2,1)}) %all-reduce.6.cloned.1.call-update) | async-done | bytes 1048592 | tf_op jit(solution)/shard_map/psum | solution.py:117
  689.1 4.0 multiply_add_fusion.2
  694.4 1.5 convolution_convert_fusion.3
  695.9 1.8 copy.96
  697.7 2.4 convolution_convert_fusion.2
  700.0 1.4 fusion.21
  703.4 1.8 copy.73
  705.2 1.8 copy.72
  707.0 1.8 copy.71
  708.8 6.2 convolution_bitcast_fusion.3
  715.0 52.0 %all-reduce.8.cloned.1.call-done = f32[256,2048]{1,0:T(8,128)} async-done(((f32[256,2048]{1,0:T(8,128)}), f32[256,2048]{1,0:T(8,128)}) %all-reduce.8.cloned.1.call-update) | async-done | bytes 2097168 | tf_op jit(solution)/shard_map/psum | solution.py:174
  767.0 2.3 fusion.10
  769.3 1.3 copy.92
  770.7 4.3 fusion.32
  775.1 9.6 fusion.54
  785.7 7.5 convolution_bitcast_fusion.1
  793.4 15.0 convolution_bitcast_fusion
  808.4 1.4 copy-done.9
  809.8 1.6 copy.79
  811.4 5.5 copy.83
  816.9 1.6 copy.74
  818.5 3.0 copy.77
  821.5 5.4 copy.80
  826.9 5.4 copy.81
  832.3 3.0 reduce-scatter.16.cloned.1.call-done
  837.5 89.2 %reduce-scatter.10.cloned.1.call-done = f32[64,2048]{1,0:T(8,128)} async-done(((f32[512,2048]{1,0:T(8,128)}), f32[64,2048]{1,0:T(8,128)}) %reduce-scatter.10.cloned.1.call-update) | async-done | bytes 524304 | tf_op jit(solution)/shard_map/reduce_scatter | solution.py:182
  926.7 1.8 multiply_reduce_fusion.6
  928.5 281.8 %reduce-scatter.14.cloned.1.call-done = f32[256,2048]{1,0:T(8,128)} async-done(((f32[2048,2048]{1,0:T(8,128)}), f32[256,2048]{1,0:T(8,128)}) %reduce-scatter.14.cloned.1.call-update) | async-done | bytes 2097168 | tf_op jit(solution)/shard_map/reduce_scatter | solution.py:184
  1210.4 2.7 multiply_reduce_fusion.2
  1213.1 207.7 %reduce-scatter.8.cloned.1.call-done = f32[3,256,512]{1,2,0:T(8,128)} async-done(((f32[3,2048,512]{1,2,0:T(8,128)}), f32[3,256,512]{1,2,0:T(8,128)}) %reduce-scatter.8.cloned.1.call-update) | async-done | bytes 1572880 | tf_op jit(solution)/shard_map/reduce_scatter | solution.py:181
  1420.8 2.4 multiply_reduce_fusion.5
  1424.5 538.1 %reduce-scatter.12.cloned.1.call-done = f32[2,256,2048]{1,2,0:T(8,128)} async-done(((f32[2,2048,2048]{1,2,0:T(8,128)}), f32[2,256,2048]{1,2,0:T(8,128)}) %reduce-scatter.12.cloned.1.call-update) | async-done | bytes 4194320 | tf_op jit(solution)/shard_map/reduce_scatter | solution.py:183
  1962.6 3.9 multiply_reduce_fusion
  1967.8 3.5 fusion.9
  1971.3 39.5 %psum.31 = f32[]{:T(128)} all-reduce(f32[]{:T(128)S(6)} %add.181), channel_id=1, replica_groups=mesh['dp'=8,'tensor'=4] {'dp','tensor'}, use_global_device_ids=true, to_apply=%region_20.21 | all-reduce | flops 1 | bytes 8 | tf_op jit(solution)/shard_map/psum | solution.py:194
  2011.5 5.7 multiply_subtract_fusion.2
  2017.2 3.0 copy.84
  2020.2 11.3 multiply_subtract_fusion
  2031.6 5.3 copy.85
  2036.9 3.0 copy.86
  2039.9 5.3 copy.87
  2045.3 1.6 copy.88
  2046.9 5.5 copy.89
  2053.0 2.6 multiply_subtract_fusion.3
  2055.7 6.1 multiply_subtract_fusion.1
  (94 shorter events, 12.8 us)
Async XLA Ops:
  7.2 2.7 copy-start.11
  7.2 3.5 copy-start.20
  7.2 26.2 %copy-start.2 = (bf16[256,2048]{1,0:T(8,128)(2,1)S(1)}, bf16[256,2048]{1,0:T(8,128)(2,1)}, u32[]{:S(2)}) copy-start(bf16[256,2048]{1,0:T(8,128)(2,1)} %param.18) | copy-start | bytes 3145732
  7.2 26.5 %copy-start.21 = (s32[1,256]{1,0:T(1,128)S(1)}, s32[1,256]{1,0:T(1,128)}, u32[]{:S(2)}) copy-start(s32[1,256]{1,0:T(1,128)} %param.19) | copy-start | bytes 3076
  7.2 105.0 %all-gather.7.cloned.1.call-start = ((), (), s32[]{:S(2)}) async-start(), calls=%async_computation.5 | async-start | bytes 7077888 | tf_op jit(solution)/shard_map/all_gather | solution.py:78
  9.8 152.5 %all-gather.9.cloned.1.call-start = ((), (), s32[]{:S(2)}) async-start(), calls=%async_computation.6 | async-start | bytes 2359296 | tf_op jit(solution)/shard_map/all_gather | solution.py:79
  10.6 205.5 %all-reduce.4.cloned.1.call-start = ((), (), s32[]{:S(2)}) async-start(), calls=%async_computation.7 | async-start | bytes 4194304 | tf_op jit(solution)/shard_map/psum | solution.py:109
  117.1 0.8 copy-start.16
  117.2 0.7 copy-start.18
  117.3 0.7 copy-start.10
  118.0 1.0 copy-start.3
  166.0 280.1 %all-gather.11.cloned.1.call-start = ((), (), s32[]{:S(2)}) async-start(), calls=%async_computation.8 | async-start | bytes 18874368 | tf_op jit(solution)/shard_map/all_gather | solution.py:80
  169.9 1.7 copy-start.6
  169.9 401.4 %all-gather.13.cloned.1.call-start = ((), (), s32[]{:S(2)}) async-start(), calls=%async_computation.9 | async-start | bytes 9437184 | tf_op jit(solution)/shard_map/all_gather | solution.py:81
  172.7 477.2 %all-gather.15.cloned.1.call-start = ((), (), s32[]{:S(2)}) async-start(), calls=%async_computation.16 | async-start | bytes 10485760 | tf_op jit(solution)/shard_map/all_gather | solution.py:129
  593.2 95.9 %all-reduce.6.cloned.1.call-start = ((), (), s32[]{:S(2)}) async-start(), calls=%async_computation.10 | async-start | bytes 2097152 | tf_op jit(solution)/shard_map/psum | solution.py:117
  600.3 166.7 %all-reduce.8.cloned.1.call-start = ((), (), s32[]{:S(2)}) async-start(), calls=%async_computation.11 | async-start | bytes 4194304 | tf_op jit(solution)/shard_map/psum | solution.py:174
  689.1 5.3 copy-start.5
  693.1 1.3 copy-start
  697.7 2.4 copy-start.4
  697.7 3.8 copy-start.17
  697.7 4.7 copy-start.19
  715.0 120.3 %reduce-scatter.16.cloned.1.call-start = ((), (), s32[]{:S(2)}) async-start(), calls=%async_computation.17 | async-start | bytes 1179648
  770.6 156.1 %reduce-scatter.10.cloned.1.call-start = ((), (), s32[]{:S(2)}) async-start(), calls=%async_computation.13 | async-start | bytes 4718592 | tf_op jit(solution)/shard_map/reduce_scatter | solution.py:182
  775.0 435.3 %reduce-scatter.14.cloned.1.call-start = ((), (), s32[]{:S(2)}) async-start(), calls=%async_computation.15 | async-start | bytes 18874368 | tf_op jit(solution)/shard_map/reduce_scatter | solution.py:184
  784.7 0.9 copy-start.15
  784.8 636.1 %reduce-scatter.8.cloned.1.call-start = ((), (), s32[]{:S(2)}) async-start(), calls=%async_computation.12 | async-start | bytes 14155776 | tf_op jit(solution)/shard_map/reduce_scatter | solution.py:181
  793.2 1169.5 %reduce-scatter.12.cloned.1.call-start = ((), (), s32[]{:S(2)}) async-start(), calls=%async_computation.14 | async-start | bytes 37748736 | tf_op jit(solution)/shard_map/reduce_scatter | solution.py:183
  808.4 1.4 copy-start.9
  811.4 5.5 copy-start.14
  1424.5 543.3 %copy-start.1 = (f32[256,2048]{1,0:T(8,128)S(1)}, f32[256,2048]{1,0:T(8,128)}, u32[]{:S(2)}) copy-start(f32[256,2048]{1,0:T(8,128)} %copy-done) | copy-start | bytes 6291460
  2046.9 5.5 copy-start.22
  2046.9 5.5 copy-start.23
  2046.9 6.1 copy-start.12
  2046.9 6.1 copy-start.13
  2046.9 8.8 copy-start.8
  2052.4 3.3 copy-start.7
Sparse Core Ops, SparseCore 0:
  10.8 101.4 all-gather.6
  115.0 47.3 all-gather.8
  166.1 49.9 all-reduce.3
  218.7 227.3 all-gather.10
  448.6 122.6 all-gather.12
  593.4 56.4 all-gather.14
  652.8 36.2 all-reduce.5
  715.1 51.8 all-reduce.7
  771.0 64.2 reduce-scatter.15
  839.3 87.3 reduce-scatter.9
  930.5 279.7 reduce-scatter.13
  1213.8 206.9 reduce-scatter.7
  1424.6 538.0 reduce-scatter.11
